TPU v7x, 32 devices: a whole 2x2x4 slice. The times are simulated.
32 devices in a mesh: seq: 8 (over z, y), view: 4 (over x, core).
Axes of the slice: x: 2, y: 2, z: 4, core: 2. Of those that a mesh axis runs over, the one named last changes fastest.
Arguments:
- ssd_input: bfloat16 [8, 4, 512, 2048], P('seq', 'view'), may hold values from -21 to 21
- gate_input: bfloat16 [8, 4, 512, 2048], P('seq', 'view'), may hold values from -6 to 6
- b_matrix: bfloat16 [8, 4, 512, 128], P('seq', 'view'), may hold values from -6 to 6
- c_matrix: bfloat16 [8, 4, 512, 128], P('seq', 'view'), may hold values from -0.52734375 to 0.52734375
- log_decay: float32 [8, 4, 32, 512], P('seq', 'view'), may hold values from -1 to 0, as said below
- d_skip: float32 [32], replicated, may hold values from 1 to 4
- norm_gain: float32 [2048], replicated, may hold values from 0.1 to 1.9
- out_weight: bfloat16 [2048, 1536], replicated, may hold values from -0.125 to 0.125
- view_order: int32 [8, 4], P('seq'), may hold values from 0 to 3, each once within a row
- tile_order: int32 [8, 4], P('seq'), may hold values from 0 to 3, each once within a row
Outputs:
- next_tokens: bfloat16 [8, 4, 512, 1536], P('seq', 'view')
Inputs may be any that keep to these rules, and one draw needn't show every extreme that they name: `log_decay`: negative everywhere. `view_order`: each row is a permutation of the views. `tile_order`: each row is a permutation of the tiles of a block.
All inputs are finite; a program needn't handle non-finite values.
Results may differ from a plain program's by a relative error of at most 0.0059.
Values may be sent and summed in bfloat16 or wider, within the bound.
A program may use at most 128 MiB of HBM per device.

v0:
```python
import functools

import jax
import jax.numpy as jnp
from jax import lax
from jax.experimental import pallas as pl
from jax.experimental.pallas import tpu as pltpu
from jax.sharding import PartitionSpec as P

GROUP = 256
TILE = 128
EPS = 1e-05
MESH = pl.DeviceIdType.MESH
F32 = jnp.float32
BF16 = jnp.bfloat16
VMEM = pltpu.VMEM
VMEM_LIMIT = 64 * 1000 * 1000


def nn(a, b):
    return lax.dot_general(a, b, (((1,), (0,)), ((), ())), preferred_element_type=F32)


def nt(a, b):
    return lax.dot_general(a, b, (((1,), (1,)), ((), ())), preferred_element_type=F32)


def tn(a, b):
    return lax.dot_general(a, b, (((0,), (0,)), ((), ())), preferred_element_type=F32)


def split3(a):
    hi = a.astype(BF16)
    rest = a - hi.astype(F32)
    mid = rest.astype(BF16)
    low = (rest - mid.astype(F32)).astype(BF16)
    return hi, mid, low


def iota(shape, dim):
    return lax.broadcasted_iota(jnp.int32, shape, dim)


def pair_columns(full, pair):
    lanes = full.shape[1]
    turned = pltpu.roll(full, lax.rem(lanes - 2 * pair, lanes), 1)
    return turned[:, 0:1], turned[:, 1:2]


def mixer_kernel(
    views, pack, groups, share, bands,
    order_ref, skip_ref, b_ref, c_ref, ld_ref, gain_ref, x_hbm, gate_hbm, w_hbm,
    out_hbm,
    x_s, inside_s, gate_s, w_s, sem_x, sem_g, sem_w, sem_o,
    col_ref, row_ref, score_ref, scale_s, total_s, state_ref, prefix_ref, ent_s,
    note_s, got_s, gotnote_s, agg_s, aggnote_s, aggs_s, aggnotes_s, within_s, before_s, send_s,
    sem_a, sem_an, sem_b, sem_bn, sem_c,
    ecol_s, entry_s, normed_s, mine_s, sem,
):
    band, view = lax.axis_index("seq"), lax.axis_index("view")
    count = views * pack
    group, member = band // pack, lax.rem(band, pack)
    me = member * views + view
    rows = share * 64
    heads, tokens = ld_ref.shape
    spans = tokens // GROUP
    pairs = x_s.shape[1] // 128
    first_half = iota((GROUP, 128), 1) < 64
    top_half = iota((128, 128), 0) < 64

    load = pltpu.make_async_copy(x_hbm, x_s, sem_x)
    load_gate = pltpu.make_async_copy(gate_hbm, gate_s, sem_g)
    load_w = pltpu.make_async_copy(w_hbm, w_s, sem_w)
    load.start()
    load_gate.start()
    load_w.start()

    barrier = pltpu.get_barrier_semaphore()
    for d in range(1, bands):
        pl.semaphore_signal(
            barrier, inc=1,
            device_id={"seq": lax.rem(band + d, bands), "view": view}, device_id_type=MESH,
        )
    for d in range(1, views):
        for m in range(pack):
            pl.semaphore_signal(
                barrier, inc=1,
                device_id={"seq": group * pack + m, "view": lax.rem(view + d, views)},
                device_id_type=MESH,
            )

    at_row, at_col = iota((GROUP, GROUP), 0), iota((GROUP, GROUP), 1)
    lower = jnp.where(at_col <= at_row, 1.0, 0.0).astype(BF16)
    upper = jnp.where(at_row <= at_col, 1.0, 0.0).astype(BF16)
    total = jnp.zeros((heads, 1), F32)
    for c in range(spans):
        span = slice(c * GROUP, (c + 1) * GROUP)
        own = ld_ref[:, span]
        padded = jnp.concatenate([own, jnp.zeros((128 - heads, GROUP), F32)], axis=0)
        lines = sum(nn(part, upper) for part in split3(own))
        row_ref[:, span] = lines
        cols = sum(nt(lower, part) for part in split3(padded))
        col_ref[span, :] = cols
        ecol_s[span, :] = jnp.exp(cols)
        scale_s[span, :] = jnp.exp(jnp.minimum(cols[GROUP - 1 : GROUP, :] - cols, 0.0))
        total = total + lines[:, GROUP - 1 : GROUP]
        scores = nt(c_ref[span, :], b_ref[span, :])
        score_ref[c] = jnp.where(at_col <= at_row, scores, 0.0)
    total_s[...] = jnp.broadcast_to(total, total_s.shape)

    rank = jnp.int32(0)
    for r in range(views):
        rank = rank + jnp.where(order_ref[0, r] == view, r, 0)
    key = (rank + member * views).astype(F32)
    for q in range(count):
        note_s[q, 0:share, :] = total_s[q * share : (q + 1) * share, :]
        note_s[q, share : share + 1, :] = jnp.full((1, 128), key, F32)

    def states_of(q):
        for j in range(share // 2):
            pair = q * (share // 2) + j
            at = slice(j * 128, (j + 1) * 128)
            lanes = pl.ds(pl.multiple_of(pair * 128, 128), 128)
            f0, f1 = pair_columns(scale_s[...], pair)
            running = jnp.zeros((128, 128), F32)
            for c in range(spans):
                span = slice(c * GROUP, (c + 1) * GROUP)
                bf = b_ref[span, :].astype(F32)
                scaled = jnp.concatenate(
                    [(f0[span, :] * bf).astype(BF16), (f1[span, :] * bf).astype(BF16)], axis=1
                )
                both = tn(x_s[span, lanes], scaled)
                state = jnp.where(top_half, both[:, 0:128], both[:, 128:256])
                if c:
                    prefix_ref[c - 1, lanes, :] = running
                e0 = row_ref[pl.ds(2 * pair, 1), span][:, GROUP - 1 : GROUP]
                e1 = row_ref[pl.ds(2 * pair + 1, 1), span][:, GROUP - 1 : GROUP]
                running = jnp.exp(jnp.where(top_half, e0, e1)) * running + state
            state_ref[q, at, :] = running.astype(BF16)

    cuts = [0, pairs * 3 // 8, pairs * 11 // 16, pairs]
    def inside_span(part):
        @pl.loop(cuts[part], cuts[part + 1])
        def _(pair):
            cols = pair_columns(col_ref[...], pair)
            lanes = pl.ds(pl.multiple_of(pair * 128, 128), 128)
            for c in range(x_s.shape[0] // GROUP):
                span = slice(c * GROUP, (c + 1) * GROUP)
                x = x_s[span, lanes]
                outs = []
                for j, col in enumerate(cols):
                    line = row_ref[pl.ds(2 * pair + j, 1), span]
                    gap = jnp.minimum(col[span, :] - line, 0.0)
                    outs.append(nn((jnp.exp(gap) * score_ref[c]).astype(BF16), x))
                inside_s[span, lanes] = (
                    jnp.where(first_half, outs[0], outs[1])
                    + jnp.where(first_half, skip_ref[2 * pair], skip_ref[2 * pair + 1]) * x.astype(F32)
                )

    def peer(q):
        return {"seq": group * pack + q // views, "view": lax.rem(q, views)}

    def across(g):
        return {"seq": g * pack + member, "view": view}

    def exchange(source, target, sem, d, q):
        return pltpu.make_async_remote_copy(
            src_ref=source, dst_ref=target, send_sem=sem.at[0, d], recv_sem=sem.at[1, d],
            device_id=peer(q), device_id_type=MESH,
        )

    sends = []
    load.wait()
    pl.semaphore_wait(barrier, bands - 1 + (views - 1) * pack)
    for d in range(1, count):
        q = lax.rem(me + d, count)
        sends.append(exchange(note_s.at[q], gotnote_s.at[me], sem_an, d, q))
        sends[-1].start()
        states_of(q)
        sends.append(exchange(state_ref.at[q], got_s.at[me], sem_a, d, q))
        sends[-1].start()
    states_of(me)
    got_s[me] = state_ref[me]
    gotnote_s[me] = note_s[me]
    inside_span(0)
    for d in range(1, count):
        src = lax.rem(me - d + count, count)
        exchange(note_s.at[src], gotnote_s.at[src], sem_an, d, src).wait_recv()
        exchange(state_ref.at[src], got_s.at[src], sem_a, d, src).wait_recv()

    logs = [gotnote_s[b] for b in range(count)]
    keys = [jnp.broadcast_to(log[share : share + 1, :], log.shape) for log in logs]
    zero = jnp.zeros_like(logs[0])
    before, upto, whole = [], [], zero
    for b in range(count):
        acc = zero
        for o in range(count):
            if o != b:
                acc = acc + jnp.where(keys[o] < keys[b], logs[o], 0.0)
        before.append(acc)
        upto.append(acc + logs[b])
        before_s[b] = jnp.exp(acc)
        whole = whole + logs[b]
    aggnote_s[...] = whole
    last = [jnp.exp(jnp.minimum(whole - upto[b], 0.0)) for b in range(count)]
    for i in range(share):
        span = slice(i * 64, (i + 1) * 64)
        acc = jnp.zeros((64, 128), F32)
        for b in range(count):
            acc = acc + last[b][i : i + 1, :] * got_s[b, span, :].astype(F32)
        agg_s[span, :] = acc.astype(BF16)

    def ahead(source, target, sem, k, g):
        return pltpu.make_async_remote_copy(
            src_ref=source, dst_ref=target, send_sem=sem.at[0, k], recv_sem=sem.at[1, k],
            device_id=across(g), device_id_type=MESH,
        )

    def ahead_pair(k, g):
        return (
            ahead(aggnote_s, aggnotes_s.at[k], sem_bn, k, g),
            ahead(agg_s, aggs_s.at[k], sem_b, k, g),
        )

    for k in range(groups - 1, 0, -1):
        @pl.when(group + k < groups)
        def _(k=k):
            for copy in ahead_pair(k, group + k):
                copy.start()

    for b in range(count):
        coefs = [
            jnp.where(
                keys[o] < keys[b], jnp.exp(jnp.minimum(before[b] - upto[o], 0.0)), 0.0
            )
            for o in range(count)
            if o != b
        ]
        others = [o for o in range(count) if o != b]
        for i in range(share):
            span = slice(i * 64, (i + 1) * 64)
            acc = jnp.zeros((64, 128), F32)
            for o, coef in zip(others, coefs):
                acc = acc + coef[i : i + 1, :] * got_s[o, span, :].astype(F32)
            within_s[b, span, :] = acc

    inside_span(1)
    carry = within_s.at[count]
    carry[...] = jnp.zeros((rows, 128), F32)
    for k in range(groups - 1, 0, -1):
        @pl.when(group - k >= 0)
        def _(k=k):
            for copy in ahead_pair(k, group - k):
                copy.wait_recv()
            decay = jnp.exp(aggnotes_s[k])
            for i in range(share):
                span = slice(i * 64, (i + 1) * 64)
                carry[span, :] = decay[i : i + 1, :] * carry[span, :] + aggs_s[k, span, :].astype(F32)

    def entering(q):
        factor = before_s[q]
        parts = []
        for i in range(share):
            span = slice(i * 64, (i + 1) * 64)
            parts.append(factor[i : i + 1, :] * carry[span, :] + within_s[q, span, :])
        return jnp.concatenate(parts, axis=0).astype(BF16)

    for d in range(1, count):
        q = lax.rem(me + d, count)
        send_s[d] = entering(q)
        sends.append(exchange(send_s.at[d], ent_s.at[me], sem_c, d, q))
        sends[-1].start()
    ent_s[me] = entering(me)
    inside_span(2)
    for d in range(1, count):
        src = lax.rem(me - d + count, count)
        exchange(send_s.at[d], ent_s.at[src], sem_c, d, src).wait_recv()
    tokens, width = inside_s.shape
    width_out = w_s.shape[1]
    piece = mine_s.shape[1]
    chunk = max(piece, TILE)
    chunks = tokens // chunk
    per_chunk = chunk // piece
    shift = (1 - band // (bands // 2)) * (chunks // 2)

    def chunk_of(i):
        return lax.rem(shift + i, chunks)

    def rows_of(i):
        return pl.ds(pl.multiple_of(chunk_of(i) * chunk, chunk), chunk)

    def to(j):
        return {"seq": j, "view": view}

    @pl.loop(0, pairs)
    def _(pair):
        rows = pl.ds(pl.multiple_of(pair * 128, 128), 128)
        per = share // 2
        mine = ent_s[pair // per, pl.ds(pl.multiple_of(lax.rem(pair, per) * 128, 128), 128), :]
        entry_s[0, rows, :] = mine
        before = jnp.ones((128, 128), F32)
        for c in range(1, spans):
            e0, e1 = pair_columns(ecol_s[c * GROUP - 8 : c * GROUP, :], pair)
            before = before * jnp.where(top_half, e0[7:8, :], e1[7:8, :])
            entry = before * mine.astype(F32) + prefix_ref[c - 1, rows, :]
            entry_s[c, rows, :] = entry.astype(BF16)

    load_gate.wait()
    def send(j):
        return pltpu.make_async_remote_copy(
            src_ref=mine_s.at[j], dst_ref=out_hbm.at[band],
            send_sem=sem.at[0, j], recv_sem=sem.at[1, band],
            device_id=to(j), device_id_type=MESH,
        )

    def arrival(i):
        return pltpu.make_async_remote_copy(
            src_ref=mine_s.at[i], dst_ref=out_hbm.at[i],
            send_sem=sem.at[0, i], recv_sem=sem.at[1, i],
            device_id=to(i), device_id_type=MESH,
        )

    half = iota((chunk, 128), 1) < 64
    same = (iota((128, 128), 0) < 64) == (iota((128, 128), 1) < 64)
    block = jnp.where(same, 1.0 / 64.0, 0.0).astype(BF16)
    for i in range(chunks):
        rows = rows_of(i)
        part = chunk_of(i) * chunk // GROUP
        def one(pair):
            lanes = pl.ds(pl.multiple_of(pair * 128, 128), 128)
            e0, e1 = pair_columns(ecol_s[rows, :], pair)
            carried = nt(c_ref[rows, :], entry_s[part, lanes, :])
            carried = carried * jnp.where(half, e0, e1)
            gate = gate_s[rows, lanes].astype(F32)
            g = (inside_s[rows, lanes] + carried) * (gate / (1.0 + jnp.exp(-gate)))
            square = g * g
            high = square.astype(BF16)
            low = (square - high.astype(F32)).astype(BF16)
            mean = nn(high, block) + nn(low, block)
            normed = g * lax.rsqrt(mean + EPS) * gain_ref[:, lanes]
            normed_s[:, lanes] = normed.astype(BF16)

        @pl.loop(0, pairs // 4)
        def _(quad):
            for k in range(4):
                one(quad * 4 + k)

        if i == 0:
            load_w.wait()
        base = chunk_of(i) * per_chunk

        @pl.loop(0, width_out // 256)
        def _(n):
            cols = pl.ds(pl.multiple_of(n * 256, 256), 256)
            made = nn(normed_s[...], w_s[:, cols])
            for u in range(per_chunk):
                mine_s[base + u, :, cols] = made[u * piece : (u + 1) * piece, :].astype(BF16)

        for u in range(per_chunk):
            j = base + u

            @pl.when(j != band)
            def _(j=j):
                send(j).start()

    keep = pltpu.make_async_copy(mine_s.at[band], out_hbm.at[band], sem_o)
    keep.start()
    for d in range(1, bands):
        arrival(lax.rem(band - d + bands, bands)).wait_recv()
    for copy in sends:
        copy.wait_send()
    for step in range(1, groups):
        @pl.when(group + step < groups)
        def _(step=step):
            for copy in ahead_pair(step, group + step):
                copy.wait_send()
    for d in range(1, bands):
        send(lax.rem(band + d, bands)).wait_send()
    keep.wait()


def mixer_part(order, skip, b, c, ld, gain, x, gate, w, views, bands):
    heads, tokens = ld.shape
    width, width_out = w.shape
    pack = 2 if bands % 2 == 0 and heads % (4 * views) == 0 else 1
    count = views * pack
    share = heads // count
    groups = bands // pack
    rows = share * 64
    piece = tokens // bands
    spans = tokens // GROUP
    vmem = pl.BlockSpec(memory_space=pltpu.VMEM)
    hbm = pl.BlockSpec(memory_space=pl.ANY)
    smem = pl.BlockSpec(memory_space=pltpu.SMEM)
    dma = pltpu.SemaphoreType.DMA
    sems = lambda n: dma((2, n))
    return pl.pallas_call(
        functools.partial(mixer_kernel, views, pack, groups, share, bands),
        in_specs=[smem] * 2 + [vmem] * 4 + [hbm] * 3,
        out_specs=hbm,
        out_shape=jax.ShapeDtypeStruct((bands, piece, width_out), BF16),
        scratch_shapes=[
            VMEM(x.shape, BF16),
            VMEM(x.shape, F32),
            VMEM(x.shape, BF16),
            VMEM(w.shape, BF16),
            dma, dma, dma, dma,
            VMEM((tokens, 128), F32),
            VMEM((heads, tokens), F32),
            VMEM((spans, GROUP, GROUP), F32),
            VMEM((tokens, 128), F32),
            VMEM((heads, 128), F32),
            VMEM((count, rows, 128), BF16),
            VMEM((spans - 1, width, 128), F32),
            VMEM((count, rows, 128), BF16),
            VMEM((count, 8, 128), F32),
            VMEM((count, rows, 128), BF16),
            VMEM((count, 8, 128), F32),
            VMEM((rows, 128), BF16),
            VMEM((8, 128), F32),
            VMEM((groups, rows, 128), BF16),
            VMEM((groups, 8, 128), F32),
            VMEM((count + 1, rows, 128), F32),
            VMEM((count, 8, 128), F32),
            VMEM((count, rows, 128), BF16),
            sems(count), sems(count), sems(groups), sems(groups), sems(count),
            VMEM((tokens, 128), F32),
            VMEM((spans, width, 128), BF16),
            VMEM((max(piece, TILE), width), BF16),
            VMEM((bands, piece, width_out), BF16),
            sems(bands),
        ],
        compiler_params=pltpu.CompilerParams(
            collective_id=0, has_side_effects=True, vmem_limit_bytes=VMEM_LIMIT
        ),
        name="mixer_part",
    )(order, skip, b, c, ld, gain, x, gate, w)


def tile_kernel(order_ref, in_ref, out_ref):
    out_ref[...] = in_ref[...]


def tile_part(order, pieces):
    bands, piece, width = pieces.shape
    per = TILE // piece
    block = (per, piece, width)
    return pl.pallas_call(
        tile_kernel,
        grid_spec=pltpu.PrefetchScalarGridSpec(
            num_scalar_prefetch=1,
            grid=(bands // per,),
            in_specs=[pl.BlockSpec(block, lambda k, order: (order[k], 0, 0))],
            out_specs=pl.BlockSpec(block, lambda k, order: (k, 0, 0)),
        ),
        out_shape=jax.ShapeDtypeStruct(pieces.shape, BF16),
        compiler_params=pltpu.CompilerParams(vmem_limit_bytes=VMEM_LIMIT),
        name="tile_part",
    )(order, pieces)


def shards(
    ssd_input, gate_input, b_matrix, c_matrix, log_decay,
    d_skip, norm_gain, out_weight, view_order, tile_order,
):
    views, bands = lax.axis_size("view"), lax.axis_size("seq")
    x, gate = ssd_input[0, 0], gate_input[0, 0]
    b, c, ld = b_matrix[0, 0], c_matrix[0, 0], log_decay[0, 0]
    tokens, width = x.shape
    pieces = mixer_part(
        view_order, d_skip, b, c, ld, norm_gain[None, :], x, gate, out_weight, views, bands
    )
    out = tile_part(tile_order[0], pieces)
    return out.reshape(1, 1, tokens, out_weight.shape[1])


def solution(mesh):
    whole = P("seq", "view", None, None)
    in_specs = (whole,) * 5 + (P(), P(), P(), P("seq", None), P("seq", None))
    return jax.shard_map(
        shards, mesh=mesh, in_specs=in_specs, out_specs=whole, check_vma=False
    )
```

profile of v0, /device:TPU:13, one launch (start us, length us, event | category | flops | bytes accessed | tf_op | source)
XLA Modules:
  0.0 77.0 jit_solution(5865204525412472851)
XLA Ops:
  0.0 72.7 %mixer_part.1.in_ref = bf16[8,64,1536]{2,1,0:T(8,128)(2,1)} custom-call(s32[1,4]{1,0:T(1,128)} %order_ref.1, f32[32]{0:T(128)} %skip_ref.1, bf16[512,128]{1,0:T(8,128)(2,1)} %bitcast.10, bf16[512,128]{1,0:T(8,128)(2,1)} %bitcast.11, f32[32,512]{1,0:T(8,128)} %bitcast.12, f32[1,2048]{1,0:T(1,128)} %bitcast.13, bf16[512,2048]{1,0:T(8,128)(2,1)} %bitcast.8, ...), custom_call_target="tpu_custom_call" | custom-call | tf_op jit(solution)/shard_map/mixer_part/pallas_call | solution.py:397
  72.7 4.2 %tile_part.1 = bf16[8,64,1536]{2,1,0:T(8,128)(2,1)} custom-call(s32[4]{0:T(128)} %bitcast.14, bf16[8,64,1536]{2,1,0:T(8,128)(2,1)} %mixer_part.1.in_ref), custom_call_target="tpu_custom_call" | custom-call | tf_op jit(solution)/shard_map/tile_part/pallas_call | solution.py:448
where the time goes:
time: 77.2 us; the launch traced here: 77 us
  Pallas kernels  77 us (100%)
    pallas_call x1, Pallas kernels, mixer_part(): pl.pallas_call(functools.partial(mixer_kernel, views, pack, groups, share...  72.7 us
    pallas_call x1, Pallas kernels, tile_part(): pl.pallas_call(tile_kernel, grid_spec=pltpu.PrefetchScalarGridSpec(num_sc...  4.24 us

commit v1 on v0

v1 whole, which is shorter than its diff:
```python
import functools
import math

import jax
import jax.numpy as jnp
from jax import lax
from jax.experimental import pallas as pl
from jax.experimental.pallas import tpu as pltpu
from jax.sharding import PartitionSpec as P

GROUP = 256
TILE = 128
EPS = 1e-05
LOG2E = math.log2(math.e)
MESH = pl.DeviceIdType.MESH
F32 = jnp.float32
BF16 = jnp.bfloat16
VMEM = pltpu.VMEM
VMEM_LIMIT = 48 * 1000 * 1000


def nn(a, b):
    return lax.dot_general(a, b, (((1,), (0,)), ((), ())), preferred_element_type=F32)


def nt(a, b):
    return lax.dot_general(a, b, (((1,), (1,)), ((), ())), preferred_element_type=F32)


def split2(a):
    hi = a.astype(BF16)
    return hi, (a - hi.astype(F32)).astype(BF16)


def split3(a):
    hi = a.astype(BF16)
    rest = a - hi.astype(F32)
    mid = rest.astype(BF16)
    low = (rest - mid.astype(F32)).astype(BF16)
    return hi, mid, low


def iota(shape, dim):
    return lax.broadcasted_iota(jnp.int32, shape, dim)


def pair_columns(full, pair):
    lanes = full.shape[1]
    turned = pltpu.roll(full, lax.rem(lanes - 2 * pair, lanes), 1)
    return turned[:, 0:1], turned[:, 1:2]


def spread(first, width):
    row = iota((256, width), 0)
    head = jnp.where(row < 128, row, row - 128)
    return jnp.where(head == first + (iota((256, width), 1) >> 6), 1.0, 0.0).astype(BF16)


def mixer_kernel(
    views, pack, groups, batches, bands,
    order_ref, skip_ref, b_ref, c_ref, ld_ref, gain_ref, x_hbm, gate_hbm, w_hbm,
    out_hbm,
    x_s, gate_s, w_s, p_s, q_s, sem_x, sem_g, sem_w, sem_o,
    col_ref, row_ref, score_ref, bt_s, scale2_s, ecol2_s, dec_s, total_s, prefix_s,
    note_s, gotnote_s, aggnote_s, aggnotes_s, coef_s, before_s, last_s,
    state_s, got_s, agg_s, aggs_s, within_s, carry_s, send_s, ent_s,
    sem_n, sem_a, sem_bn, sem_b, sem_c,
    entry_s, normed_s, mine_s, sem,
):
    band, view = lax.axis_index("seq"), lax.axis_index("view")
    count = views * pack
    chips = count // 2
    group, member = band // pack, lax.rem(band, pack)
    me = member * views + view
    heads, tokens = ld_ref.shape
    spans = tokens // GROUP
    width = x_s.shape[1]
    pairs = width // 128
    HALF = GROUP // 2

    load = pltpu.make_async_copy(x_hbm, x_s, sem_x)
    load_gate = pltpu.make_async_copy(gate_hbm, gate_s, sem_g)
    load_w = pltpu.make_async_copy(w_hbm, w_s, sem_w)
    load.start()
    load_gate.start()
    load_w.start()

    barrier = pltpu.get_barrier_semaphore()
    for d in range(1, bands):
        pl.semaphore_signal(
            barrier, inc=1,
            device_id={"seq": lax.rem(band + d, bands), "view": view}, device_id_type=MESH,
        )
    for d in range(1, views):
        for m in range(pack):
            pl.semaphore_signal(
                barrier, inc=1,
                device_id={"seq": group * pack + m, "view": lax.rem(view + d, views)},
                device_id_type=MESH,
            )

    at_row, at_col = iota((GROUP, GROUP), 0), iota((GROUP, GROUP), 1)
    lower = jnp.where(at_col <= at_row, 1.0, 0.0).astype(BF16)
    upper = jnp.where(at_row <= at_col, 1.0, 0.0).astype(BF16)
    total = jnp.zeros((heads, 1), F32)
    for c in range(spans):
        span = slice(c * GROUP, (c + 1) * GROUP)
        own = ld_ref[:, span] * LOG2E
        padded = jnp.concatenate([own, jnp.zeros((128 - heads, GROUP), F32)], axis=0)
        lines = sum(nn(part, upper) for part in split3(own))
        row_ref[:, span] = lines
        cols = sum(nt(lower, part) for part in split3(padded))
        col_ref[span, :] = cols
        for ref, value in (
            (ecol2_s, jnp.exp2(cols)),
            (scale2_s, jnp.exp2(jnp.minimum(cols[GROUP - 1 : GROUP, :] - cols, 0.0))),
        ):
            hi, lo = split2(value)
            ref[span, 0:128] = hi
            ref[span, 128:256] = lo
        total = total + lines[:, GROUP - 1 : GROUP]
        bt_s[:, span] = b_ref[span, :].astype(F32).T.astype(BF16)
    total_s[...] = jnp.broadcast_to(total, total_s.shape)

    rank = jnp.int32(0)
    for r in range(views):
        rank = rank + jnp.where(order_ref[0, r] == view, r, 0)
    key = (rank + member * views).astype(F32)
    left = iota((1, 128), 1) < 64
    for q in range(count):
        for j in range(batches):
            head = 2 * (j * count + q)
            note_s[q, j : j + 1, :] = jnp.where(
                left, total_s[head : head + 1, :], total_s[head + 1 : head + 2, :]
            )
        note_s[q, batches : batches + 1, :] = jnp.full((1, 128), key, F32)

    def peer(q):
        return {"seq": group * pack + q // views, "view": lax.rem(q, views)}

    def exchange(source, target, sends, receives, q):
        return pltpu.make_async_remote_copy(
            src_ref=source, dst_ref=target, send_sem=sends, recv_sem=receives,
            device_id=peer(q), device_id_type=MESH,
        )

    def note_copy(q, slot):
        return exchange(note_s.at[q], gotnote_s.at[slot], sem_n.at[0, q], sem_n.at[1, slot], q)

    def state_copy(j, q, slot):
        return exchange(
            state_s.at[j, q], got_s.at[j, slot], sem_a.at[j, 0, q], sem_a.at[j, 1, slot], q
        )

    def enter_copy(j, q, slot):
        return exchange(
            send_s.at[j, q], ent_s.at[j, slot], sem_c.at[j, 0, q], sem_c.at[j, 1, slot], q
        )

    def others():
        return [lax.rem(me + d, count) for d in range(1, count)]

    def ahead(source, target, sems, k, g):
        return pltpu.make_async_remote_copy(
            src_ref=source, dst_ref=target, send_sem=sems.at[0, k], recv_sem=sems.at[1, k],
            device_id={"seq": g * pack + member, "view": view}, device_id_type=MESH,
        )

    def aggnote_copy(k, g):
        return ahead(aggnote_s, aggnotes_s.at[k], sem_bn, k, g)

    def agg_copy(j, k, g):
        return ahead(agg_s.at[j], aggs_s.at[j, k], sem_b.at[j], k, g)

    def later(run):
        for k in range(groups - 1, 0, -1):
            @pl.when(group + k < groups)
            def _(k=k):
                run(k, group + k)

    def earlier(run):
        for k in range(groups - 1, 0, -1):
            @pl.when(group - k >= 0)
            def _(k=k):
                run(k, group - k)

    pl.semaphore_wait(barrier, bands - 1 + (views - 1) * pack)
    for q in others():
        note_copy(q, me).start()

    def states(j, chip):
        base = j * count + 2 * chip
        lanes = pl.ds(pl.multiple_of(base * 128, 256), 256)
        pick = spread(2 * base, 256)
        running = jnp.zeros((128, 256), F32)
        for c in range(spans):
            span = slice(c * GROUP, (c + 1) * GROUP)
            scale = nn(scale2_s[span, :], pick)
            made = nn(bt_s[:, span], (x_s[span, lanes].astype(F32) * scale).astype(BF16))
            ends = nn(ecol2_s[(c + 1) * GROUP - 16 : (c + 1) * GROUP, :], pick)
            dec = ends[15:16, :]
            prefix_s[c, :, lanes] = running
            dec_s[c, :, lanes] = jnp.broadcast_to(dec, (8, 256))
            running = dec * running + made if c else made
        for i in range(2):
            state_s[j, 2 * chip + i] = running[:, i * 128 : (i + 1) * 128].astype(BF16)

    mychip = me // 2
    partner = me + 1 - 2 * lax.rem(me, 2)
    load.wait()
    for j in range(batches):
        for d in range(1, chips):
            chip = lax.rem(mychip + d, chips)
            states(j, chip)
            for i in range(2):
                state_copy(j, 2 * chip + i, me).start()
        states(j, mychip)
        state_copy(j, partner, me).start()
        got_s[j, me] = state_s[j, me]

    for c in range(spans):
        span = slice(c * GROUP, (c + 1) * GROUP)
        scores = nt(c_ref[span, :], b_ref[span, :])
        score_ref[c] = jnp.where(at_col <= at_row, scores, 0.0)

    first_half = iota((GROUP, 128), 1) < 64

    def inside_span(start, stop):
        @pl.loop(start, stop)
        def _(pair):
            cols = pair_columns(col_ref[...], pair)
            lanes = pl.ds(pl.multiple_of(pair * 128, 128), 128)
            pick = spread(2 * pair, 128)
            for c in range(spans):
                span = slice(c * GROUP, (c + 1) * GROUP)
                x = x_s[span, lanes]
                outs = []
                for j, col in enumerate(cols):
                    line = row_ref[pl.ds(2 * pair + j, 1), span]
                    col = col[span, :]
                    top = jnp.minimum(col[:HALF] - line[:, :HALF], 0.0)
                    top = (jnp.exp2(top) * score_ref[c, :HALF, :HALF]).astype(BF16)
                    low = jnp.minimum(col[HALF:] - line, 0.0)
                    low = (jnp.exp2(low) * score_ref[c, HALF:, :]).astype(BF16)
                    outs.append(jnp.concatenate([nn(top, x[:HALF]), nn(low, x)], axis=0))
                gate = gate_s[span, lanes].astype(F32)
                silu = gate / (1.0 + jnp.exp(-gate))
                q_s[span, lanes] = nn(ecol2_s[span, :], pick) * silu
                made = jnp.where(first_half, outs[0], outs[1]) + jnp.where(
                    first_half, skip_ref[2 * pair], skip_ref[2 * pair + 1]
                ) * x.astype(F32)
                p_s[span, lanes] = made * silu

    cuts = CUTS(pairs)
    load_gate.wait()
    inside_span(cuts[0], cuts[1])

    gotnote_s[me] = note_s[me]
    for q in others():
        note_copy(q, q).wait_recv()
    logs = [gotnote_s[b] for b in range(count)]
    keys = [jnp.broadcast_to(log[batches : batches + 1, :], log.shape) for log in logs]
    zero = jnp.zeros_like(logs[0])
    upto, whole = [], zero
    for b in range(count):
        acc = zero
        for o in range(count):
            if o != b:
                acc = acc + jnp.where(keys[o] < keys[b], logs[o], 0.0)
        upto.append(acc + logs[b])
        before_s[b] = jnp.exp2(acc)
        for o in range(count):
            coef_s[b, o] = acc
        whole = whole + logs[b]
    aggnote_s[...] = whole
    later(lambda k, g: aggnote_copy(k, g).start())
    for b in range(count):
        last_s[b] = jnp.exp2(jnp.minimum(whole - upto[b], 0.0))
        for o in range(count):
            if o != b:
                coef_s[b, o] = jnp.where(
                    keys[o] < keys[b], jnp.exp2(jnp.minimum(coef_s[b, o] - upto[o], 0.0)), 0.0
                )

    for j in range(batches):
        for q in others():
            state_copy(j, q, q).wait_recv()
        for i in range(4):
            part = slice(i * 32, (i + 1) * 32)
            acc = jnp.zeros((32, 128), F32)
            for b in range(count):
                acc = acc + last_s[b, j : j + 1, :] * got_s[j, b, part, :].astype(F32)
            agg_s[j, part, :] = acc.astype(BF16)
        later(lambda k, g: agg_copy(j, k, g).start())
        for i in range(4):
            part = slice(i * 32, (i + 1) * 32)
            blocks = [got_s[j, o, part, :].astype(F32) for o in range(count)]
            for b in range(count):
                acc = jnp.zeros((32, 128), F32)
                for o in range(count):
                    if o != b:
                        acc = acc + coef_s[b, o, j : j + 1, :] * blocks[o]
                within_s[j, b, part, :] = acc

    inside_span(cuts[1], cuts[2])

    earlier(lambda k, g: aggnote_copy(k, g).wait_recv())
    for j in range(batches):
        carry_s[...] = jnp.zeros_like(carry_s)

        def gather(k, g):
            agg_copy(j, k, g).wait_recv()
            decay = jnp.exp2(aggnotes_s[k, j : j + 1, :])
            carry_s[...] = decay * carry_s[...] + aggs_s[j, k].astype(F32)

        earlier(gather)

        def entering(q):
            return (before_s[q, j : j + 1, :] * carry_s[...] + within_s[j, q]).astype(BF16)

        for q in others():
            send_s[j, q] = entering(q)
            enter_copy(j, q, me).start()
        ent_s[j, me] = entering(me)

    inside_span(cuts[2], cuts[3])

    piece = mine_s.shape[1]
    width_out = w_s.shape[1]
    chunk = normed_s.shape[0]
    chunks = tokens // chunk
    half = chunks // 2
    per_chunk = chunk // piece
    turn = lax.rem(band // per_chunk, half)
    mine_half = band // (bands // 2)
    same = (iota((256, 256), 0) >> 6) == (iota((256, 256), 1) >> 6)
    block = jnp.where(same, 1.0 / 64.0, 0.0).astype(BF16)
    quads = width // 256

    def send(j):
        return pltpu.make_async_remote_copy(
            src_ref=mine_s.at[j], dst_ref=out_hbm.at[band],
            send_sem=sem.at[0, j], recv_sem=sem.at[1, band],
            device_id={"seq": j, "view": view}, device_id_type=MESH,
        )

    def arrival(i):
        return pltpu.make_async_remote_copy(
            src_ref=mine_s.at[i], dst_ref=out_hbm.at[i],
            send_sem=sem.at[0, i], recv_sem=sem.at[1, i],
            device_id={"seq": i, "view": view}, device_id_type=MESH,
        )

    def entry_of(c, j):
        for q in range(count):
            at = (j * count + q) * 128
            lanes = slice(at, at + 128)
            made = ent_s[j, q].astype(F32)
            entry_s[:, lanes] = (before_of(c, lanes) * made + prefix_s[c, :, lanes]).astype(BF16)

    def before_of(c, lanes):
        made = jnp.ones((1, lanes.stop - lanes.start), F32)
        for o in range(spans - 1):
            made = made * jnp.where(o < c, dec_s[o, 0:1, lanes], 1.0)
        return made

    def gated(rows, quad):
        lanes = slice(quad * 256, (quad + 1) * 256)
        carried = nn(c_ref[rows, :], entry_s[:, lanes])
        g = p_s[rows, lanes] + q_s[rows, lanes] * carried
        high, low = split2(g * g)
        mean = nn(high, block) + nn(low, block)
        normed_s[:, lanes] = (g * lax.rsqrt(mean + EPS) * gain_ref[:, lanes]).astype(BF16)

    def project(index):
        for n in range(width_out // 256):
            cols = slice(n * 256, (n + 1) * 256)
            made = nn(normed_s[...], w_s[:, cols]).astype(BF16)
            for u in range(per_chunk):
                mine_s[index * per_chunk + u, :, cols] = made[u * piece : (u + 1) * piece, :]
        for u in range(per_chunk):
            j = index * per_chunk + u

            @pl.when(j != band)
            def _(j=j):
                send(j).start()

    def rows_of(index):
        return pl.ds(pl.multiple_of(index * chunk, chunk), chunk)

    for side in range(2):
        base = (1 - mine_half if side == 0 else mine_half) * half
        c = base * chunk // GROUP
        if side == 0:
            for j in range(batches):
                for q in others():
                    enter_copy(j, q, q).wait_recv()
                entry_of(c, j)
            load_w.wait()
        else:
            for j in range(batches):
                entry_of(c, j)

        @pl.loop(0, half)
        def _(i, base=base, side=side):
            index = base + lax.rem(turn + i + side, half)
            for quad in range(quads):
                gated(rows_of(index), quad)
            project(index)

    keep = pltpu.make_async_copy(mine_s.at[band], out_hbm.at[band], sem_o)
    keep.start()
    for q in others():
        note_copy(q, me).wait_send()
        for j in range(batches):
            state_copy(j, q, me).wait_send()
            enter_copy(j, q, me).wait_send()
    later(lambda k, g: aggnote_copy(k, g).wait_send())
    for j in range(batches):
        later(lambda k, g: agg_copy(j, k, g).wait_send())
    for d in range(1, bands):
        arrival(lax.rem(band - d + bands, bands)).wait_recv()
    for d in range(1, bands):
        send(lax.rem(band + d, bands)).wait_send()
    keep.wait()


def CUTS(pairs):
    return [0, pairs // 2, pairs * 3 // 4, pairs]


def mixer_part(order, skip, b, c, ld, gain, x, gate, w, views, bands):
    heads, tokens = ld.shape
    width, width_out = w.shape
    pack = 2 if bands % 2 == 0 and heads % (4 * views) == 0 else 1
    count = views * pack
    batches = heads // (2 * count)
    groups = bands // pack
    piece = tokens // bands
    spans = tokens // GROUP
    vmem = pl.BlockSpec(memory_space=pltpu.VMEM)
    hbm = pl.BlockSpec(memory_space=pl.ANY)
    smem = pl.BlockSpec(memory_space=pltpu.SMEM)
    dma = pltpu.SemaphoreType.DMA
    sems = lambda *n: dma(n)
    return pl.pallas_call(
        functools.partial(mixer_kernel, views, pack, groups, batches, bands),
        in_specs=[smem] * 2 + [vmem] * 4 + [hbm] * 3,
        out_specs=hbm,
        out_shape=jax.ShapeDtypeStruct((bands, piece, width_out), BF16),
        scratch_shapes=[
            VMEM(x.shape, BF16),
            VMEM(x.shape, BF16),
            VMEM(w.shape, BF16),
            VMEM(x.shape, F32),
            VMEM(x.shape, F32),
            dma, dma, dma, dma,
            VMEM((tokens, 128), F32),
            VMEM((heads, tokens), F32),
            VMEM((spans, GROUP, GROUP), F32),
            VMEM((128, tokens), BF16),
            VMEM((tokens, 256), BF16),
            VMEM((tokens, 256), BF16),
            VMEM((spans, 8, width), F32),
            VMEM((heads, 128), F32),
            VMEM((spans, 128, width), F32),
            VMEM((count, 8, 128), F32),
            VMEM((count, 8, 128), F32),
            VMEM((8, 128), F32),
            VMEM((groups, 8, 128), F32),
            VMEM((count, count, 8, 128), F32),
            VMEM((count, 8, 128), F32),
            VMEM((count, 8, 128), F32),
            VMEM((batches, count, 128, 128), BF16),
            VMEM((batches, count, 128, 128), BF16),
            VMEM((batches, 128, 128), BF16),
            VMEM((batches, groups, 128, 128), BF16),
            VMEM((batches, count, 128, 128), F32),
            VMEM((128, 128), F32),
            VMEM((batches, count, 128, 128), BF16),
            VMEM((batches, count, 128, 128), BF16),
            sems(2, count), sems(batches, 2, count), sems(2, groups),
            sems(batches, 2, groups), sems(batches, 2, count),
            VMEM((128, width), BF16),
            VMEM((max(piece, TILE // 2), width), BF16),
            VMEM((bands, piece, width_out), BF16),
            sems(2, bands),
        ],
        compiler_params=pltpu.CompilerParams(
            collective_id=0, has_side_effects=True, vmem_limit_bytes=VMEM_LIMIT
        ),
        name="mixer_part",
    )(order, skip, b, c, ld, gain, x, gate, w)


def tile_kernel(order_ref, in_hbm, out_hbm, hold, sems):
    bands = in_hbm.shape[0]
    tiles, per = order_ref.shape[0], bands // order_ref.shape[0]

    def fetch(k):
        return pltpu.make_async_copy(
            in_hbm.at[pl.ds(order_ref[k] * per, per)], hold.at[k], sems.at[0, k]
        )

    def put(k):
        return pltpu.make_async_copy(
            hold.at[k], out_hbm.at[k * per : (k + 1) * per], sems.at[1, k]
        )

    for k in range(tiles):
        fetch(k).start()
    for k in range(tiles):
        fetch(k).wait()
        put(k).start()
    for k in range(tiles):
        put(k).wait()


def tile_part(order, pieces):
    bands, piece, width = pieces.shape
    tiles = order.shape[0]
    per = TILE // piece
    return pl.pallas_call(
        tile_kernel,
        in_specs=[
            pl.BlockSpec(memory_space=pltpu.SMEM),
            pl.BlockSpec(memory_space=pl.ANY),
        ],
        out_specs=pl.BlockSpec(memory_space=pl.ANY),
        out_shape=jax.ShapeDtypeStruct(pieces.shape, BF16),
        scratch_shapes=[
            VMEM((tiles, per, piece, width), BF16),
            pltpu.SemaphoreType.DMA((2, tiles)),
        ],
        compiler_params=pltpu.CompilerParams(vmem_limit_bytes=VMEM_LIMIT),
        name="tile_part",
    )(order, pieces)


def shards(
    ssd_input, gate_input, b_matrix, c_matrix, log_decay,
    d_skip, norm_gain, out_weight, view_order, tile_order,
):
    views, bands = lax.axis_size("view"), lax.axis_size("seq")
    x, gate = ssd_input[0, 0], gate_input[0, 0]
    b, c, ld = b_matrix[0, 0], c_matrix[0, 0], log_decay[0, 0]
    tokens, width = x.shape
    pieces = mixer_part(
        view_order, d_skip, b, c, ld, norm_gain[None, :], x, gate, out_weight, views, bands
    )
    out = tile_part(tile_order[0], pieces)
    return out.reshape(1, 1, tokens, out_weight.shape[1])


def solution(mesh):
    whole = P("seq", "view", None, None)
    in_specs = (whole,) * 5 + (P(), P(), P(), P("seq", None), P("seq", None))
    return jax.shard_map(
        shards, mesh=mesh, in_specs=in_specs, out_specs=whole, check_vma=False
    )
```

time: 77.2 us -> 77.8 us (level)
  the two profiles are of different devices: /device:TPU:13 before, /device:TPU:0 now
where the time goes in v1:
time: 77.8 us; the launch traced here: 77.5 us
  Pallas kernels  69.6 us (89%)
  local copies, waits for them, and re-layouts  7.84 us (10%)
    pallas_call x1, Pallas kernels, mixer_part(): pl.pallas_call(functools.partial(mixer_kernel, views, pack, groups, batch...  67.1 us
    unnamed x18, local copies, waits for them, and re-layouts  7.84 us
    pallas_call x1, Pallas kernels, tile_part(): pl.pallas_call(tile_kernel, in_specs=[pl.BlockSpec(memory_space=pltpu.SME...  2.51 us

profile of v1, /device:TPU:0, one launch (start us, length us, event | category | flops | bytes accessed | tf_op | source)
XLA Modules:
  0.0 77.5 jit_solution(13540570954745739623)
XLA Ops:
  0.0 0.0 copy-start
  0.0 1.6 %copy-done = bf16[1,1,512,2048]{3,2,1,0:T(8,128)(2,1)S(1)} copy-done((bf16[1,1,512,2048]{3,2,1,0:T(8,128)(2,1)S(1)}, bf16[1,1,512,2048]{3,2,1,0:T(8,128)(2,1)}, u32[]{:S(2)}) %copy-start) | copy-done | bytes 2097176
  1.6 0.0 copy-start.1
  1.6 1.6 %copy-done.1 = bf16[1,1,512,2048]{3,2,1,0:T(8,128)(2,1)S(1)} copy-done((bf16[1,1,512,2048]{3,2,1,0:T(8,128)(2,1)S(1)}, bf16[1,1,512,2048]{3,2,1,0:T(8,128)(2,1)}, u32[]{:S(2)}) %copy-start.1) | copy-done | bytes 2097176
  3.2 0.0 copy-start.2
  3.2 0.9 %copy-done.2 = bf16[1,1,512,128]{3,2,1,0:T(8,128)(2,1)S(1)} copy-done((bf16[1,1,512,128]{3,2,1,0:T(8,128)(2,1)S(1)}, bf16[1,1,512,128]{3,2,1,0:T(8,128)(2,1)}, u32[]{:S(2)}) %copy-start.2) | copy-done | bytes 131096
  4.1 0.0 copy-start.3
  4.1 0.9 %copy-done.3 = bf16[1,1,512,128]{3,2,1,0:T(8,128)(2,1)S(1)} copy-done((bf16[1,1,512,128]{3,2,1,0:T(8,128)(2,1)S(1)}, bf16[1,1,512,128]{3,2,1,0:T(8,128)(2,1)}, u32[]{:S(2)}) %copy-start.3) | copy-done | bytes 131096
  5.0 0.0 copy-start.4
  5.0 0.8 %copy-done.4 = f32[1,1,32,512]{3,2,1,0:T(8,128)S(1)} copy-done((f32[1,1,32,512]{3,2,1,0:T(8,128)S(1)}, f32[1,1,32,512]{3,2,1,0:T(8,128)}, u32[]{:S(2)}) %copy-start.4) | copy-done | bytes 65560
  5.8 0.0 copy-start.5
  5.8 0.7 copy-done.5
  6.5 0.0 copy-start.6
  6.5 0.7 copy-done.6
  7.2 0.0 copy-start.7
  7.2 0.7 copy-done.7
  7.8 0.0 copy-start.8
  7.8 67.1 %mixer_part.1.in_hbm = bf16[8,64,1536]{2,1,0:T(8,128)(2,1)S(1)} custom-call(s32[1,4]{1,0:T(1,128)S(1)} %copy-done.6, f32[32]{0:T(128)S(1)} %copy-done.7, bf16[512,128]{1,0:T(8,128)(2,1)S(1)} %bitcast.10, bf16[512,128]{1,0:T(8,128)(2,1)S(1)} %bitcast.11, f32[32,512]{1,0:T(8,128)S(1)} %bitcast.12, f32[1,2048]{1,0:T(1,128)S(1)} %bitcast.13, ...), custom_call_target="tpu_custom_call" | custom-call | tf_op jit(solution)/shard_map/mixer_part/pallas_call | solution.py:446
  75.0 0.0 copy-done.8
  75.0 2.5 %tile_part.1 = bf16[8,64,1536]{2,1,0:T(8,128)(2,1)} custom-call(s32[4]{0:T(128)S(1)} %bitcast.14, bf16[8,64,1536]{2,1,0:T(8,128)(2,1)S(1)} %mixer_part.1.in_hbm), custom_call_target="tpu_custom_call" | custom-call | tf_op jit(solution)/shard_map/tile_part/pallas_call | solution.py:523
Async XLA Ops:
  0.0 1.6 %copy-start = (bf16[1,1,512,2048]{3,2,1,0:T(8,128)(2,1)S(1)}, bf16[1,1,512,2048]{3,2,1,0:T(8,128)(2,1)}, u32[]{:S(2)}) copy-start(bf16[1,1,512,2048]{3,2,1,0:T(8,128)(2,1)} %param.10) | copy-start | bytes 6291460
  1.6 1.6 %copy-start.1 = (bf16[1,1,512,2048]{3,2,1,0:T(8,128)(2,1)S(1)}, bf16[1,1,512,2048]{3,2,1,0:T(8,128)(2,1)}, u32[]{:S(2)}) copy-start(bf16[1,1,512,2048]{3,2,1,0:T(8,128)(2,1)} %param.11) | copy-start | bytes 6291460
  3.2 0.9 %copy-start.2 = (bf16[1,1,512,128]{3,2,1,0:T(8,128)(2,1)S(1)}, bf16[1,1,512,128]{3,2,1,0:T(8,128)(2,1)}, u32[]{:S(2)}) copy-start(bf16[1,1,512,128]{3,2,1,0:T(8,128)(2,1)} %param.12) | copy-start | bytes 393220
  4.1 0.9 %copy-start.3 = (bf16[1,1,512,128]{3,2,1,0:T(8,128)(2,1)S(1)}, bf16[1,1,512,128]{3,2,1,0:T(8,128)(2,1)}, u32[]{:S(2)}) copy-start(bf16[1,1,512,128]{3,2,1,0:T(8,128)(2,1)} %param.13) | copy-start | bytes 393220
  5.0 0.8 %copy-start.4 = (f32[1,1,32,512]{3,2,1,0:T(8,128)S(1)}, f32[1,1,32,512]{3,2,1,0:T(8,128)}, u32[]{:S(2)}) copy-start(f32[1,1,32,512]{3,2,1,0:T(8,128)} %param.14) | copy-start | bytes 196612
  5.8 0.7 copy-start.5
  6.5 0.7 copy-start.6
  7.2 0.7 copy-start.7
  7.8 67.1 %copy-start.8 = (s32[1,4]{1,0:T(1,128)S(1)}, s32[1,4]{1,0:T(1,128)}, u32[]{:S(2)}) copy-start(s32[1,4]{1,0:T(1,128)} %param.19) | copy-start | bytes 52

commit v2 on v1

--- a/solution.py
+++ b/solution.py
@@ -16,7 +16,7 @@
 F32 = jnp.float32
 BF16 = jnp.bfloat16
 VMEM = pltpu.VMEM
-VMEM_LIMIT = 48 * 1000 * 1000
+VMEM_LIMIT = 64 * 1000 * 1000
 
 
 def nn(a, b):
@@ -446,8 +446,8 @@
     return pl.pallas_call(
         functools.partial(mixer_kernel, views, pack, groups, batches, bands),
         in_specs=[smem] * 2 + [vmem] * 4 + [hbm] * 3,
-        out_specs=hbm,
-        out_shape=jax.ShapeDtypeStruct((bands, piece, width_out), BF16),
+        out_specs=vmem,
+        out_shape=VMEM((bands, piece, width_out), BF16),
         scratch_shapes=[
             VMEM(x.shape, BF16),
             VMEM(x.shape, BF16),
@@ -493,24 +493,18 @@
     )(order, skip, b, c, ld, gain, x, gate, w)
 
 
-def tile_kernel(order_ref, in_hbm, out_hbm, hold, sems):
-    bands = in_hbm.shape[0]
-    tiles, per = order_ref.shape[0], bands // order_ref.shape[0]
-
-    def fetch(k):
-        return pltpu.make_async_copy(
-            in_hbm.at[pl.ds(order_ref[k] * per, per)], hold.at[k], sems.at[0, k]
-        )
+def tile_kernel(order_ref, in_ref, out_hbm, sems):
+    tiles = order_ref.shape[0]
+    per = in_ref.shape[0] // tiles
 
     def put(k):
         return pltpu.make_async_copy(
-            hold.at[k], out_hbm.at[k * per : (k + 1) * per], sems.at[1, k]
+            in_ref.at[pl.ds(order_ref[k] * per, per)],
+            out_hbm.at[k * per : (k + 1) * per],
+            sems.at[k],
         )
 
     for k in range(tiles):
-        fetch(k).start()
-    for k in range(tiles):
-        fetch(k).wait()
         put(k).start()
     for k in range(tiles):
         put(k).wait()
@@ -519,7 +513,6 @@
 def tile_part(order, pieces):
     bands, piece, width = pieces.shape
     tiles = order.shape[0]
-    per = TILE // piece
     return pl.pallas_call(
         tile_kernel,
         in_specs=[
@@ -528,11 +521,8 @@
         ],
         out_specs=pl.BlockSpec(memory_space=pl.ANY),
         out_shape=jax.ShapeDtypeStruct(pieces.shape, BF16),
-        scratch_shapes=[
-            VMEM((tiles, per, piece, width), BF16),
-            pltpu.SemaphoreType.DMA((2, tiles)),
-        ],
-        compiler_params=pltpu.CompilerParams(vmem_limit_bytes=VMEM_LIMIT),
+        scratch_shapes=[pltpu.SemaphoreType.DMA((tiles,))],
+        compiler_params=pltpu.CompilerParams(vmem_limit_bytes=VMEM_LIMIT // 16),
         name="tile_part",
     )(order, pieces)
 

time: 77.8 us -> 69.2 us (0.89)
  local copies, waits for them, and re-layouts: 7.84 us -> 0.01 us
    unnamed x18 -> x2, local copies, waits for them, and re-layouts: 7.84 us -> 0.01 us
    pallas_call x1, Pallas kernels: 2.51 us -> 1.71 us  [tile_part(): pl.pallas_call(tile_kernel, in_specs=[pl.BlockSpec(memory_space=pltpu.SME...]
where the time goes in v2:
time: 69.2 us; the launch traced here: 69 us
  Pallas kernels  69 us (100%)
    pallas_call x1, Pallas kernels, mixer_part(): pl.pallas_call(functools.partial(mixer_kernel, views, pack, groups, batch...  67.3 us
    pallas_call x1, Pallas kernels, tile_part(): pl.pallas_call(tile_kernel, in_specs=[pl.BlockSpec(memory_space=pltpu.SME...  1.71 us

profile of v2, /device:TPU:0, one launch (start us, length us, event | category | flops | bytes accessed | tf_op | source)
XLA Modules:
  0.0 69.0 jit_solution(2688536320987261754)
XLA Ops:
  0.0 0.0 copy-start
  0.0 67.3 %mixer_part.1.in_ref = bf16[8,64,1536]{2,1,0:T(8,128)(2,1)S(1)} custom-call(s32[1,4]{1,0:T(1,128)} %order_ref.1, f32[32]{0:T(128)} %skip_ref.1, bf16[512,128]{1,0:T(8,128)(2,1)} %bitcast.11, bf16[512,128]{1,0:T(8,128)(2,1)} %bitcast.12, f32[32,512]{1,0:T(8,128)} %bitcast.13, f32[1,2048]{1,0:T(1,128)} %bitcast.14, bf16[512,2048]{1,0:T(8,128)(2,1)} %bitcast.9, ...), custom_call_target="tpu_custom_call" | custom-call | tf_op jit(solution)/shard_map/mixer_part/pallas_call | solution.py:446
  67.3 0.0 copy-done
  67.3 1.7 %tile_part.1 = bf16[8,64,1536]{2,1,0:T(8,128)(2,1)} custom-call(s32[4]{0:T(128)S(1)} %bitcast.8, bf16[8,64,1536]{2,1,0:T(8,128)(2,1)S(1)} %mixer_part.1.in_ref), custom_call_target="tpu_custom_call" | custom-call | tf_op jit(solution)/shard_map/tile_part/pallas_call | solution.py:516
Async XLA Ops:
  0.0 67.3 %copy-start = (s32[1,4]{1,0:T(1,128)S(1)}, s32[1,4]{1,0:T(1,128)}, u32[]{:S(2)}) copy-start(s32[1,4]{1,0:T(1,128)} %param.19) | copy-start | bytes 52

commit v3 on v2

--- a/solution.py
+++ b/solution.py
@@ -64,8 +64,8 @@
     col_ref, row_ref, score_ref, bt_s, scale2_s, ecol2_s, dec_s, total_s, prefix_s,
     note_s, gotnote_s, aggnote_s, aggnotes_s, coef_s, before_s, last_s,
     state_s, got_s, agg_s, aggs_s, within_s, carry_s, send_s, ent_s,
-    sem_n, sem_a, sem_bn, sem_b, sem_c,
-    entry_s, normed_s, mine_s, sem,
+    sem_n, sem_a, sem_bn, sem_b, sem_c, pre_s, pregot_s, sem_p,
+    entry_s, normed_s, made_s, mine_s, sem,
 ):
     band, view = lax.axis_index("seq"), lax.axis_index("view")
     count = views * pack
@@ -157,8 +157,16 @@
             send_s.at[j, q], ent_s.at[j, slot], sem_c.at[j, 0, q], sem_c.at[j, 1, slot], q
         )
 
+    mychip = me // 2
+    partner = me + 1 - 2 * lax.rem(me, 2)
+
+    def far_chips():
+        if chips == 4:
+            return [3 - mychip, lax.rem(mychip + 2, 4), mychip + 1 - 2 * lax.rem(mychip, 2)]
+        return [lax.rem(mychip + d, chips) for d in range(1, chips)]
+
     def others():
-        return [lax.rem(me + d, count) for d in range(1, count)]
+        return [2 * chip + i for chip in far_chips() for i in range(2)] + [partner]
 
     def ahead(source, target, sems, k, g):
         return pltpu.make_async_remote_copy(
@@ -172,17 +180,26 @@
     def agg_copy(j, k, g):
         return ahead(agg_s.at[j], aggs_s.at[j, k], sem_b.at[j], k, g)
 
+    even = lax.rem(group, 2) == 0
+
     def later(run):
         for k in range(groups - 1, 0, -1):
-            @pl.when(group + k < groups)
+            @pl.when((group + k < groups) & (lax.rem(group + k, 2) == 0))
             def _(k=k):
                 run(k, group + k)
 
     def earlier(run):
         for k in range(groups - 1, 0, -1):
-            @pl.when(group - k >= 0)
+            @pl.when((group - k >= 0) & even)
             def _(k=k):
                 run(k, group - k)
+
+    def prefix_copy(j, g):
+        return pltpu.make_async_remote_copy(
+            src_ref=pre_s.at[j], dst_ref=pregot_s.at[j],
+            send_sem=sem_p.at[0, j], recv_sem=sem_p.at[1, j],
+            device_id={"seq": g * pack + member, "view": view}, device_id_type=MESH,
+        )
 
     pl.semaphore_wait(barrier, bands - 1 + (views - 1) * pack)
     for q in others():
@@ -205,12 +222,9 @@
         for i in range(2):
             state_s[j, 2 * chip + i] = running[:, i * 128 : (i + 1) * 128].astype(BF16)
 
-    mychip = me // 2
-    partner = me + 1 - 2 * lax.rem(me, 2)
     load.wait()
     for j in range(batches):
-        for d in range(1, chips):
-            chip = lax.rem(mychip + d, chips)
+        for chip in far_chips():
             states(j, chip)
             for i in range(2):
                 state_copy(j, 2 * chip + i, me).start()
@@ -315,6 +329,17 @@
 
         earlier(gather)
 
+        @pl.when(jnp.logical_not(even))
+        def _(j=j):
+            prefix_copy(j, group - 1).wait_recv()
+            carry_s[...] = pregot_s[j].astype(F32)
+
+        @pl.when(even & (group + 1 < groups))
+        def _(j=j):
+            decay = jnp.exp2(aggnote_s[j : j + 1, :])
+            pre_s[j] = (decay * carry_s[...] + agg_s[j].astype(F32)).astype(BF16)
+            prefix_copy(j, group + 1).start()
+
         def entering(q):
             return (before_s[q, j : j + 1, :] * carry_s[...] + within_s[j, q]).astype(BF16)
 
@@ -333,6 +358,14 @@
     per_chunk = chunk // piece
     turn = lax.rem(band // per_chunk, half)
     mine_half = band // (bands // 2)
+
+    def far_index(i):
+        pair = i // 2
+        f = (1 - mine_half) * (half // 2 - 1 - pair) + mine_half * pair
+        return (1 - mine_half) * half + 2 * f + lax.rem(turn + i, 2)
+
+    def near_index(i):
+        return mine_half * half + lax.rem(turn + 1 + i, half)
     same = (iota((256, 256), 0) >> 6) == (iota((256, 256), 1) >> 6)
     block = jnp.where(same, 1.0 / 64.0, 0.0).astype(BF16)
     quads = width // 256
@@ -372,10 +405,13 @@
         mean = nn(high, block) + nn(low, block)
         normed_s[:, lanes] = (g * lax.rsqrt(mean + EPS) * gain_ref[:, lanes]).astype(BF16)
 
-    def project(index):
+    def project(index, split=0):
         for n in range(width_out // 256):
             cols = slice(n * 256, (n + 1) * 256)
-            made = nn(normed_s[...], w_s[:, cols]).astype(BF16)
+            made = nn(normed_s[:, split:], w_s[split:, cols])
+            if split:
+                made = made + made_s[:, cols]
+            made = made.astype(BF16)
             for u in range(per_chunk):
                 mine_s[index * per_chunk + u, :, cols] = made[u * piece : (u + 1) * piece, :]
         for u in range(per_chunk):
@@ -388,25 +424,41 @@
     def rows_of(index):
         return pl.ds(pl.multiple_of(index * chunk, chunk), chunk)
 
-    for side in range(2):
-        base = (1 - mine_half if side == 0 else mine_half) * half
-        c = base * chunk // GROUP
-        if side == 0:
-            for j in range(batches):
-                for q in others():
-                    enter_copy(j, q, q).wait_recv()
-                entry_of(c, j)
+    lead = quads // batches
+    split = (batches - 1) * lead * 256
+    first = far_index(0)
+    c = first * chunk // GROUP
+    for j in range(batches):
+        for q in others():
+            enter_copy(j, q, q).wait_recv()
+        entry_of(c, j)
+        for quad in range(j * lead, (j + 1) * lead):
+            gated(rows_of(first), quad)
+        if j == batches - 2:
             load_w.wait()
-        else:
-            for j in range(batches):
-                entry_of(c, j)
-
-        @pl.loop(0, half)
-        def _(i, base=base, side=side):
-            index = base + lax.rem(turn + i + side, half)
-            for quad in range(quads):
-                gated(rows_of(index), quad)
-            project(index)
+            for n in range(width_out // 256):
+                cols = slice(n * 256, (n + 1) * 256)
+                made_s[:, cols] = nn(normed_s[:, :split], w_s[:split, cols])
+    if batches == 1:
+        load_w.wait()
+    project(first, split)
+
+    @pl.loop(1, half)
+    def _(i):
+        index = far_index(i)
+        for quad in range(quads):
+            gated(rows_of(index), quad)
+        project(index)
+
+    for j in range(batches):
+        entry_of(mine_half * half * chunk // GROUP, j)
+
+    @pl.loop(0, half)
+    def _(i):
+        index = near_index(i)
+        for quad in range(quads):
+            gated(rows_of(index), quad)
+        project(index)
 
     keep = pltpu.make_async_copy(mine_s.at[band], out_hbm.at[band], sem_o)
     keep.start()
@@ -418,6 +470,11 @@
     later(lambda k, g: aggnote_copy(k, g).wait_send())
     for j in range(batches):
         later(lambda k, g: agg_copy(j, k, g).wait_send())
+
+        @pl.when(even & (group + 1 < groups))
+        def _(j=j):
+            prefix_copy(j, group + 1).wait_send()
+
     for d in range(1, bands):
         arrival(lax.rem(band - d + bands, bands)).wait_recv()
     for d in range(1, bands):
@@ -481,8 +538,12 @@
             VMEM((batches, count, 128, 128), BF16),
             sems(2, count), sems(batches, 2, count), sems(2, groups),
             sems(batches, 2, groups), sems(batches, 2, count),
+            VMEM((batches, 128, 128), BF16),
+            VMEM((batches, 128, 128), BF16),
+            sems(2, batches),
             VMEM((128, width), BF16),
             VMEM((max(piece, TILE // 2), width), BF16),
+            VMEM((max(piece, TILE // 2), width_out), F32),
             VMEM((bands, piece, width_out), BF16),
             sems(2, bands),
         ],

time: 69.2 us -> 63.9 us (0.923)
  the two profiles are of different devices: /device:TPU:0 before, /device:TPU:13 now
where the time goes in v3:
time: 63.9 us; the launch traced here: 62.9 us
  Pallas kernels  62.9 us (98%)
    pallas_call x1, Pallas kernels, mixer_part(): pl.pallas_call(functools.partial(mixer_kernel, views, pack, groups, batch...  61.2 us
    pallas_call x1, Pallas kernels, tile_part(): pl.pallas_call(tile_kernel, in_specs=[pl.BlockSpec(memory_space=pltpu.SME...  1.71 us

profile of v3, /device:TPU:13, one launch (start us, length us, event | category | flops | bytes accessed | tf_op | source)
XLA Modules:
  0.0 62.9 jit_solution(15793627137360353677)
XLA Ops:
  0.0 0.0 copy-start
  0.0 61.2 %mixer_part.1.in_ref = bf16[8,64,1536]{2,1,0:T(8,128)(2,1)S(1)} custom-call(s32[1,4]{1,0:T(1,128)} %order_ref.1, f32[32]{0:T(128)} %skip_ref.1, bf16[512,128]{1,0:T(8,128)(2,1)} %bitcast.11, bf16[512,128]{1,0:T(8,128)(2,1)} %bitcast.12, f32[32,512]{1,0:T(8,128)} %bitcast.13, f32[1,2048]{1,0:T(1,128)} %bitcast.14, bf16[512,2048]{1,0:T(8,128)(2,1)} %bitcast.9, ...), custom_call_target="tpu_custom_call" | custom-call | tf_op jit(solution)/shard_map/mixer_part/pallas_call | solution.py:503
  61.2 0.0 copy-done
  61.2 1.7 %tile_part.1 = bf16[8,64,1536]{2,1,0:T(8,128)(2,1)} custom-call(s32[4]{0:T(128)S(1)} %bitcast.8, bf16[8,64,1536]{2,1,0:T(8,128)(2,1)S(1)} %mixer_part.1.in_ref), custom_call_target="tpu_custom_call" | custom-call | tf_op jit(solution)/shard_map/tile_part/pallas_call | solution.py:577
Async XLA Ops:
  0.0 61.2 %copy-start = (s32[1,4]{1,0:T(1,128)S(1)}, s32[1,4]{1,0:T(1,128)}, u32[]{:S(2)}) copy-start(s32[1,4]{1,0:T(1,128)} %param.19) | copy-start | bytes 52

commit v4 on v3

--- a/solution.py
+++ b/solution.py
@@ -265,7 +265,7 @@
                 ) * x.astype(F32)
                 p_s[span, lanes] = made * silu
 
-    cuts = CUTS(pairs)
+    cuts = fill_cuts(pairs, batches)
     load_gate.wait()
     inside_span(cuts[0], cuts[1])
 
@@ -315,8 +315,7 @@
                     if o != b:
                         acc = acc + coef_s[b, o, j : j + 1, :] * blocks[o]
                 within_s[j, b, part, :] = acc
-
-    inside_span(cuts[1], cuts[2])
+        inside_span(cuts[j + 1], cuts[j + 2])
 
     earlier(lambda k, g: aggnote_copy(k, g).wait_recv())
     for j in range(batches):
@@ -347,8 +346,7 @@
             send_s[j, q] = entering(q)
             enter_copy(j, q, me).start()
         ent_s[j, me] = entering(me)
-
-    inside_span(cuts[2], cuts[3])
+        inside_span(cuts[batches + j + 1], cuts[batches + j + 2])
 
     piece = mine_s.shape[1]
     width_out = w_s.shape[1]
@@ -482,8 +480,11 @@
     keep.wait()
 
 
-def CUTS(pairs):
-    return [0, pairs // 2, pairs * 3 // 4, pairs]
+def fill_cuts(pairs, batches):
+    shares = [4, 2, 1, 2, 7]
+    if batches != 2:
+        shares = [1] * (2 * batches + 1)
+    return [pairs * sum(shares[:i]) // sum(shares) for i in range(len(shares) + 1)]
 
 
 def mixer_part(order, skip, b, c, ld, gain, x, gate, w, views, bands):

time: 63.9 us -> 62.7 us (0.981)
  Pallas kernels: 62.9 us -> 61.5 us
    pallas_call x1, Pallas kernels: 61.2 us -> 59.8 us  [mixer_part(): pl.pallas_call(functools.partial(mixer_kernel, views, pack, groups, batch...]
where the time goes in v4:
time: 62.7 us; the launch traced here: 61.6 us
  Pallas kernels  61.5 us (98%)
    pallas_call x1, Pallas kernels, mixer_part(): pl.pallas_call(functools.partial(mixer_kernel, views, pack, groups, batch...  59.8 us
    pallas_call x1, Pallas kernels, tile_part(): pl.pallas_call(tile_kernel, in_specs=[pl.BlockSpec(memory_space=pltpu.SME...  1.71 us

profile of v4, /device:TPU:13, one launch (start us, length us, event | category | flops | bytes accessed | tf_op | source)
XLA Modules:
  0.0 61.6 jit_solution(4842224182906992804)
XLA Ops:
  0.0 0.0 copy-start
  0.0 59.8 %mixer_part.1.in_ref = bf16[8,64,1536]{2,1,0:T(8,128)(2,1)S(1)} custom-call(s32[1,4]{1,0:T(1,128)} %order_ref.1, f32[32]{0:T(128)} %skip_ref.1, bf16[512,128]{1,0:T(8,128)(2,1)} %bitcast.11, bf16[512,128]{1,0:T(8,128)(2,1)} %bitcast.12, f32[32,512]{1,0:T(8,128)} %bitcast.13, f32[1,2048]{1,0:T(1,128)} %bitcast.14, bf16[512,2048]{1,0:T(8,128)(2,1)} %bitcast.9, ...), custom_call_target="tpu_custom_call" | custom-call | tf_op jit(solution)/shard_map/mixer_part/pallas_call | solution.py:504
  59.8 0.0 copy-done
  59.8 1.7 %tile_part.1 = bf16[8,64,1536]{2,1,0:T(8,128)(2,1)} custom-call(s32[4]{0:T(128)S(1)} %bitcast.8, bf16[8,64,1536]{2,1,0:T(8,128)(2,1)S(1)} %mixer_part.1.in_ref), custom_call_target="tpu_custom_call" | custom-call | tf_op jit(solution)/shard_map/tile_part/pallas_call | solution.py:578
Async XLA Ops:
  0.0 59.8 %copy-start = (s32[1,4]{1,0:T(1,128)S(1)}, s32[1,4]{1,0:T(1,128)}, u32[]{:S(2)}) copy-start(s32[1,4]{1,0:T(1,128)} %param.19) | copy-start | bytes 52

commit v5 on v4

--- a/solution.py
+++ b/solution.py
@@ -58,9 +58,9 @@
 
 def mixer_kernel(
     views, pack, groups, batches, bands,
-    order_ref, skip_ref, b_ref, c_ref, ld_ref, gain_ref, x_hbm, gate_hbm, w_hbm,
+    order_ref, skip_ref, b_hbm, c_hbm, ld_hbm, gain_hbm, x_hbm, gate_hbm, w_hbm,
     out_hbm,
-    x_s, gate_s, w_s, p_s, q_s, sem_x, sem_g, sem_w, sem_o,
+    b_ref, c_ref, ld_ref, gain_ref, sem_in, x_s, gate_s, w_s, p_s, q_s, sem_x, sem_g, sem_w, sem_o,
     col_ref, row_ref, score_ref, bt_s, scale2_s, ecol2_s, dec_s, total_s, prefix_s,
     note_s, gotnote_s, aggnote_s, aggnotes_s, coef_s, before_s, last_s,
     state_s, got_s, agg_s, aggs_s, within_s, carry_s, send_s, ent_s,
@@ -81,9 +81,16 @@
     load = pltpu.make_async_copy(x_hbm, x_s, sem_x)
     load_gate = pltpu.make_async_copy(gate_hbm, gate_s, sem_g)
     load_w = pltpu.make_async_copy(w_hbm, w_s, sem_w)
+    small = [
+        pltpu.make_async_copy(source, target, sem_in.at[i])
+        for i, (source, target) in enumerate(
+            ((ld_hbm, ld_ref), (b_hbm, b_ref), (c_hbm, c_ref), (gain_hbm, gain_ref))
+        )
+    ]
+    for copy in small:
+        copy.start()
     load.start()
     load_gate.start()
-    load_w.start()
 
     barrier = pltpu.get_barrier_semaphore()
     for d in range(1, bands):
@@ -99,6 +106,8 @@
                 device_id_type=MESH,
             )
 
+    for copy in small:
+        copy.wait()
     at_row, at_col = iota((GROUP, GROUP), 0), iota((GROUP, GROUP), 1)
     lower = jnp.where(at_col <= at_row, 1.0, 0.0).astype(BF16)
     upper = jnp.where(at_row <= at_col, 1.0, 0.0).astype(BF16)
@@ -223,6 +232,7 @@
             state_s[j, 2 * chip + i] = running[:, i * 128 : (i + 1) * 128].astype(BF16)
 
     load.wait()
+    load_w.start()
     for j in range(batches):
         for chip in far_chips():
             states(j, chip)
@@ -375,6 +385,13 @@
             device_id={"seq": j, "view": view}, device_id_type=MESH,
         )
 
+    def send_columns(j, cols):
+        return pltpu.make_async_remote_copy(
+            src_ref=mine_s.at[j, :, cols], dst_ref=out_hbm.at[band, :, cols],
+            send_sem=sem.at[0, j], recv_sem=sem.at[1, band],
+            device_id={"seq": j, "view": view}, device_id_type=MESH,
+        )
+
     def arrival(i):
         return pltpu.make_async_remote_copy(
             src_ref=mine_s.at[i], dst_ref=out_hbm.at[i],
@@ -412,7 +429,12 @@
             made = made.astype(BF16)
             for u in range(per_chunk):
                 mine_s[index * per_chunk + u, :, cols] = made[u * piece : (u + 1) * piece, :]
-        for u in range(per_chunk):
+            if split and (n % 2 == 1 or n == width_out // 256 - 1):
+                for u in range(per_chunk):
+                    send_columns(
+                        index * per_chunk + u, slice((n - n % 2) * 256, (n + 1) * 256)
+                    ).start()
+        for u in range(0 if split else per_chunk):
             j = index * per_chunk + u
 
             @pl.when(j != band)
@@ -503,10 +525,15 @@
     sems = lambda *n: dma(n)
     return pl.pallas_call(
         functools.partial(mixer_kernel, views, pack, groups, batches, bands),
-        in_specs=[smem] * 2 + [vmem] * 4 + [hbm] * 3,
+        in_specs=[smem] * 2 + [hbm] * 7,
         out_specs=vmem,
         out_shape=VMEM((bands, piece, width_out), BF16),
         scratch_shapes=[
+            VMEM(b.shape, BF16),
+            VMEM(c.shape, BF16),
+            VMEM(ld.shape, F32),
+            VMEM(gain.shape, F32),
+            sems(4),
             VMEM(x.shape, BF16),
             VMEM(x.shape, BF16),
             VMEM(w.shape, BF16),

time: 62.7 us -> 62.2 us (level)
  no operation moved by 1% of the time
where the time goes in v5:
time: 62.2 us; the launch traced here: 61.1 us
  Pallas kernels  61 us (98%)
    pallas_call x1, Pallas kernels, mixer_part(): pl.pallas_call(functools.partial(mixer_kernel, views, pack, groups, batch...  59.3 us
    pallas_call x1, Pallas kernels, tile_part(): pl.pallas_call(tile_kernel, in_specs=[pl.BlockSpec(memory_space=pltpu.SME...  1.71 us

profile of v5, /device:TPU:13, one launch (start us, length us, event | category | flops | bytes accessed | tf_op | source)
XLA Modules:
  0.0 61.1 jit_solution(11764619752056032247)
XLA Ops:
  0.0 0.0 copy-start
  0.0 59.3 %mixer_part.1.in_ref = bf16[8,64,1536]{2,1,0:T(8,128)(2,1)S(1)} custom-call(s32[1,4]{1,0:T(1,128)} %order_ref.1, f32[32]{0:T(128)} %skip_ref.1, bf16[512,128]{1,0:T(8,128)(2,1)} %bitcast.11, bf16[512,128]{1,0:T(8,128)(2,1)} %bitcast.12, f32[32,512]{1,0:T(8,128)} %bitcast.13, f32[1,2048]{1,0:T(1,128)} %bitcast.14, bf16[512,2048]{1,0:T(8,128)(2,1)} %bitcast.9, ...), custom_call_target="tpu_custom_call" | custom-call | tf_op jit(solution)/shard_map/mixer_part/pallas_call | solution.py:526
  59.3 0.0 copy-done
  59.3 1.7 %tile_part.1 = bf16[8,64,1536]{2,1,0:T(8,128)(2,1)} custom-call(s32[4]{0:T(128)S(1)} %bitcast.8, bf16[8,64,1536]{2,1,0:T(8,128)(2,1)S(1)} %mixer_part.1.in_ref), custom_call_target="tpu_custom_call" | custom-call | tf_op jit(solution)/shard_map/tile_part/pallas_call | solution.py:605
Async XLA Ops:
  0.0 59.3 %copy-start = (s32[1,4]{1,0:T(1,128)S(1)}, s32[1,4]{1,0:T(1,128)}, u32[]{:S(2)}) copy-start(s32[1,4]{1,0:T(1,128)} %param.19) | copy-start | bytes 52
